TPU v7x, 256 devices: a whole 4x4x8 slice. The times are simulated.
256 devices in a mesh: seg: 32 (over y, x, core), band: 8 (over z).
Axes of the slice: x: 4, y: 4, z: 8, core: 2. Of those that a mesh axis runs over, the one named last changes fastest.
Arguments:
- jac_first: bfloat16 [32, 4, 4096, 384], P('seg', None, 'band'), may hold values from -0.09375 to 0.09375
- jac_second: bfloat16 [32, 4, 4096, 384], P('seg', None, 'band'), may hold values from -0.013671875 to 0.013671875
- residual: bfloat16 [32, 4, 4096], P('seg', None, 'band'), may hold values from -1.25 to 1.25
- damp_inner: float32 [32, 3, 384], P('seg'), may hold values from 0.01 to 0.05
- damp_sep: float32 [32, 384], P('seg'), may hold values from 0.01 to 0.05
Outputs:
- separators: float32 [32, 384], P('seg')
- interior: float32 [32, 3, 384], P('seg')
All inputs are finite; a program needn't handle non-finite values.
Results may differ from a plain program's by a relative error of at most 0.0003.
Values may be sent and summed in bfloat16 or wider, within the bound.
No kernel may reach another device: no remote copies, remote signals or barrier semaphores. Data moves between devices by JAX's collectives and lax.ppermute only.
A program may use at most 128 MiB of HBM per device.

v0:
```python
import jax
import jax.numpy as jnp
from jax import lax
from jax.sharding import PartitionSpec as P

HIGH = lax.Precision.HIGHEST


def shifted_2(shard, axis, by):
    devices = lax.axis_size(axis)
    return lax.ppermute(shard, axis, [(i, (i + by) % devices) for i in range(devices)])


def matmul_high(left, right):
    return jnp.matmul(left, right, precision=HIGH)


def lower_solve(chol, rhs):
    return jax.scipy.linalg.solve_triangular(chol, rhs, lower=True)


def upper_solve(chol, rhs):
    return jax.scipy.linalg.solve_triangular(chol, rhs, lower=True, trans=1)


def link_tiles(first, second, resid):
    paa = jnp.einsum("lri,lrj->lij", first, first, preferred_element_type=jnp.float32)
    pab = jnp.einsum("lri,lrj->lij", first, second, preferred_element_type=jnp.float32)
    pbb = jnp.einsum("lri,lrj->lij", second, second, preferred_element_type=jnp.float32)
    grad_a = jnp.einsum("lri,lr->li", first, resid, preferred_element_type=jnp.float32)
    grad_b = jnp.einsum("lri,lr->li", second, resid, preferred_element_type=jnp.float32)
    size = paa.shape[-1]
    zero_tile = jnp.zeros((1, size, size), jnp.float32)
    zero_row = jnp.zeros((1, size), jnp.float32)
    diag = jnp.concatenate([paa, zero_tile]) + jnp.concatenate(
        [zero_tile, pbb - pab - jnp.swapaxes(pab, 1, 2) + paa]
    )
    off = pab - paa
    grad = jnp.concatenate([grad_a, zero_row]) + jnp.concatenate([zero_row, grad_b - grad_a])
    return (diag, off, grad)


def segment_complement(diag, off, grad, damp_inner, damp_sep):
    size = diag.shape[-1]
    inner = damp_inner.shape[0]
    chols, lows, zlist, wlist = ([], [], [], [])
    zero = jnp.zeros((size, size), jnp.float32)
    for k in range(inner):
        block = diag[k + 1] + jnp.diag(damp_inner[k])
        left = off[0].T if k == 0 else zero
        right = off[inner] if k == inner - 1 else zero
        couple = jnp.concatenate([left, right], axis=1)
        target = -grad[k + 1]
        if k > 0:
            block = block - matmul_high(lows[-1], lows[-1].T)
            couple = couple - matmul_high(lows[-1], zlist[-1])
            target = target - matmul_high(lows[-1], wlist[-1])
        chol = jnp.linalg.cholesky(block)
        zlist.append(lower_solve(chol, couple))
        wlist.append(lower_solve(chol, target))
        chols.append(chol)
        if k < inner - 1:
            lows.append(lower_solve(chol, off[k + 1]).T)
    top = jnp.concatenate([diag[0], zero], axis=1)
    bottom = jnp.concatenate([zero, diag[inner + 1] + jnp.diag(damp_sep)], axis=1)
    schur = jnp.concatenate([top, bottom], axis=0)
    reduced = jnp.concatenate([-grad[0], -grad[inner + 1]])
    for k in range(inner):
        schur = schur - matmul_high(zlist[k].T, zlist[k])
        reduced = reduced - matmul_high(zlist[k].T, wlist[k])
    comp = (
        schur[:size, :size],
        schur[:size, size:],
        schur[size:, size:],
        reduced[:size],
        reduced[size:],
    )
    return (comp, (chols, lows, zlist, wlist))


def back_substitute(factors, left, right):
    chols, lows, zlist, wlist = factors
    inner = len(chols)
    ends = jnp.concatenate([left, right])
    values = [wlist[k] - matmul_high(zlist[k], ends) for k in range(inner)]
    steps = [None] * inner
    steps[inner - 1] = upper_solve(chols[inner - 1], values[inner - 1])
    for k in range(inner - 2, -1, -1):
        steps[k] = upper_solve(chols[k], values[k] - matmul_high(lows[k].T, steps[k + 1]))
    return jnp.stack(steps)


def merge(first_arc, second_arc):
    all_a, alr_a, arr_a, al_a, ar_a = first_arc
    bll, blr, brr, bl, br = second_arc
    size = all_a.shape[0]
    chol = jnp.linalg.cholesky(arr_a + bll)
    couple = jnp.concatenate([alr_a.T, blr], axis=1)
    weights = jax.scipy.linalg.cho_solve((chol, True), couple)
    shifted = jax.scipy.linalg.cho_solve((chol, True), ar_a + bl)
    new_ll = all_a - matmul_high(alr_a, weights[:, :size])
    new_lr = -matmul_high(alr_a, weights[:, size:])
    new_rr = brr - matmul_high(blr.T, weights[:, size:])
    new_l = al_a - matmul_high(alr_a, shifted)
    new_r = br - matmul_high(blr.T, shifted)
    return ((new_ll, new_lr, new_rr, new_l, new_r), (weights, shifted))


def closure(arc):
    all_a, alr_a, arr_a, al_a, ar_a = arc
    whole = all_a + alr_a + alr_a.T + arr_a
    chol = jnp.linalg.cholesky(whole)
    return jax.scipy.linalg.cho_solve((chol, True), al_a + ar_a)


def shards(jac_first, jac_second, residual, damp_inner, damp_sep):
    diag_part, off_part, grad_part = link_tiles(jac_first[0], jac_second[0], residual[0])
    diag, off, grad = lax.psum((diag_part, off_part, grad_part), "band")
    comp, factors = segment_complement(diag, off, grad, damp_inner[0], damp_sep[0])
    count = lax.axis_size("seg")
    levels = count.bit_length() - 1
    arc = comp
    saved_all = []
    for level in range(levels):
        neighbour = shifted_2((arc[0], arc[1], arc[2], arc[3], arc[4]), "seg", 1 << level)
        arc, saved = merge(neighbour, arc)
        saved_all.append(saved)
    top = closure(arc)
    left = shifted_2(top, "seg", 1)
    interior = back_substitute(factors, left, top)
    return (top[None], interior[None])


def solution(mesh):
    return jax.shard_map(
        shards,
        mesh=mesh,
        in_specs=(
            P("seg", None, "band", None),
            P("seg", None, "band", None),
            P("seg", None, "band"),
            P("seg", None, None),
            P("seg", None),
        ),
        out_specs=(P("seg", None), P("seg", None, None)),
        check_vma=False,
    )
```

profile of v0, /device:TPU:6, one launch (start us, length us, event | category | flops | bytes accessed | tf_op | source)
XLA Modules:
  0.0 1482.5 jit_solution(7692737453462276813)
XLA Ops:
  29.7 34.4 %psum.23 = f32[5,384]{1,0:T(8,128)S(1)} all-reduce(f32[5,384]{1,0:T(8,128)S(1)} %pad_add_fusion.1), channel_id=1, replica_groups=mesh['seg'=32,'band'=8] {'band'}, use_global_device_ids=true, to_apply=%region_8.13 | all-reduce | flops 1920 | bytes 15360 | tf_op jit(solution)/shard_map/psum | solution.py:118
  65.3 96.8 %all-reduce.12.cloned.1.call-done = (f32[4,384,384]{2,1,0:T(8,128)}, f32[5,384,384]{1,2,0:T(8,128)}) async-done(((f32[4,384,384]{2,1,0:T(8,128)}, f32[5,384,384]{1,2,0:T(8,128)}), (f32[4,384,384]{2,1,0:T(8,128)}, f32[5,384,384]{1,2,0:T(8,128)})) %all-reduce.12.cloned.1.call-update) | async-done | bytes 5308432 | tf_op jit(solution)/shard_map/psum | solution.py:118
  167.2 11.7 cholesky.663
  190.0 11.7 cholesky.682
  212.9 11.7 cholesky.701
  233.1 29.7 %custom-call.80 = f32[3,128,128]{1,2,0:T(8,128)S(1)} custom-call(f32[3,128,128]{2,1,0:T(8,128)S(1)} %get-tuple-element.221), custom_call_target="InvertDiagBlocksLowerTriangular" | custom-call | tf_op jit(solution)/shard_map/jit(_solve_triangular)/triangular_solve/custom-call.1 | solution.py:19
  282.2 11.7 cholesky.716
  305.1 11.7 cholesky.735
  328.0 11.7 cholesky.754
  348.6 29.7 %custom-call.84 = f32[3,128,128]{1,2,0:T(8,128)S(1)} custom-call(f32[3,128,128]{2,1,0:T(8,128)S(1)} %get-tuple-element.223), custom_call_target="InvertDiagBlocksLowerTriangular" | custom-call | tf_op jit(solution)/shard_map/jit(_solve_triangular)/triangular_solve/custom-call.1 | solution.py:19
  385.9 11.7 cholesky.769
  409.9 12.1 cholesky.788
  433.2 11.7 cholesky.807
  454.3 29.7 %custom-call.88 = f32[3,128,128]{1,2,0:T(8,128)S(1)} custom-call(f32[3,128,128]{2,1,0:T(8,128)S(1)} %get-tuple-element.225), custom_call_target="InvertDiagBlocksLowerTriangular" | custom-call | tf_op jit(solution)/shard_map/jit(_solve_triangular)/triangular_solve/custom-call.1 | solution.py:19
  521.1 11.7 cholesky.822
  545.8 11.7 cholesky.841
  569.5 11.7 cholesky.860
  590.1 29.5 %custom-call.91 = f32[3,128,128]{1,2,0:T(8,128)S(1)} custom-call(f32[3,128,128]{2,1,0:T(8,128)S(1)} %get-tuple-element.226), custom_call_target="InvertDiagBlocksLowerTriangular" | custom-call | tf_op jit(solution)/shard_map/jit(_cho_solve)/triangular_solve | solution.py:99
  671.3 11.7 cholesky.875
  683.7 10.4 custom-call.93
  698.6 13.2 cholesky.894
  713.9 11.4 custom-call.94
  728.2 13.2 cholesky.913
  754.0 31.0 %custom-call.95 = f32[3,128,128]{1,2,0:T(8,128)} custom-call(f32[3,128,128]{2,1,0:T(8,128)} %get-tuple-element.228), custom_call_target="InvertDiagBlocksLowerTriangular" | custom-call | tf_op jit(solution)/shard_map/jit(_cho_solve)/triangular_solve | solution.py:99
  834.6 12.7 collective-permute-done.3
  851.2 11.7 cholesky.928
  863.6 10.4 custom-call.97
  878.6 13.2 cholesky.947
  893.9 11.5 custom-call.98
  908.1 13.2 cholesky.966
  934.1 30.9 %custom-call.99 = f32[3,128,128]{1,2,0:T(8,128)} custom-call(f32[3,128,128]{2,1,0:T(8,128)} %get-tuple-element.230), custom_call_target="InvertDiagBlocksLowerTriangular" | custom-call | tf_op jit(solution)/shard_map/jit(_cho_solve)/triangular_solve | solution.py:99
  995.6 19.3 %collective-permute-done.11 = f32[384,384]{0,1:T(8,128)S(1)} collective-permute-done((f32[384,384]{0,1:T(8,128)}, f32[384,384]{0,1:T(8,128)S(1)}, u32[]{:S(2)}, u32[]{:S(2)}) %collective-permute-start.11) | collective-permute-done | bytes 589856 | tf_op jit(solution)/shard_map/ppermute | solution.py:11
  1018.8 11.7 cholesky.981
  1031.2 10.4 custom-call.101
  1046.1 13.2 cholesky.1000
  1061.4 11.5 custom-call.102
  1075.7 13.2 cholesky.1019
  1101.6 31.0 %custom-call.103 = f32[3,128,128]{1,2,0:T(8,128)} custom-call(f32[3,128,128]{2,1,0:T(8,128)} %get-tuple-element.232), custom_call_target="InvertDiagBlocksLowerTriangular" | custom-call | tf_op jit(solution)/shard_map/jit(_cho_solve)/triangular_solve | solution.py:99
  1167.4 18.8 %collective-permute-done.14 = f32[384,384]{0,1:T(8,128)S(1)} collective-permute-done((f32[384,384]{0,1:T(8,128)}, f32[384,384]{0,1:T(8,128)S(1)}, u32[]{:S(2)}, u32[]{:S(2)}) %collective-permute-start.14) | collective-permute-done | bytes 589856 | tf_op jit(solution)/shard_map/ppermute | solution.py:11
  1199.4 11.7 cholesky.1034
  1226.7 13.2 cholesky.1053
  1242.0 11.7 custom-call.106
  1256.5 13.2 cholesky.1072
  1282.3 31.0 %custom-call.107 = f32[3,128,128]{1,2,0:T(8,128)} custom-call(f32[3,128,128]{2,1,0:T(8,128)} %get-tuple-element.234), custom_call_target="InvertDiagBlocksLowerTriangular" | custom-call | tf_op jit(solution)/shard_map/jit(_cho_solve)/triangular_solve | solution.py:99
  1349.2 11.7 cholesky.1087
  1373.8 11.9 cholesky.1106
  1397.5 11.7 cholesky.1125
  1421.7 29.5 %custom-call.125 = f32[3,128,128]{1,2,0:T(8,128)S(1)} custom-call(f32[3,128,128]{2,1,0:T(8,128)S(1)} %get-tuple-element.250), custom_call_target="InvertDiagBlocksLowerTriangular" | custom-call | tf_op jit(solution)/shard_map/jit(_cho_solve)/triangular_solve/custom-call.7 | solution.py:113
  (835 shorter events, 651.5 us)
Async XLA Ops:
  7.2 154.9 %all-reduce.12.cloned.1.call-start = ((), (), s32[]{:S(2)}) async-start(), calls=%async_computation | async-start | bytes 10616832 | tf_op jit(solution)/shard_map/psum | solution.py:118
  263.0 244.4 %copy-start.83 = (f32[128,1]{0,1:T(1,128)}, f32[128,1]{0,1:T(1,128)S(1)}, u32[]{:S(2)}) copy-start(f32[128,1]{0,1:T(1,128)S(1)} %convolution_bitcast_fusion.89) | copy-start | bytes 1540
  267.6 239.9 %copy-start.12 = (f32[128,768]{1,0:T(8,128)}, f32[128,768]{1,0:T(8,128)S(1)}, u32[]{:S(2)}) copy-start(f32[128,768]{1,0:T(8,128)S(1)} %fusion.414) | copy-start | bytes 1179652
  348.6 141.6 %copy-start.15 = (f32[384,384]{1,0:T(8,128)}, f32[384,384]{1,0:T(8,128)S(1)}, u32[]{:S(2)}) copy-start(f32[384,384]{1,0:T(8,128)S(1)} %get-tuple-element.878) | copy-start | bytes 1769476
  378.4 113.5 %copy-start.32 = (f32[3,128,128]{1,2,0:T(8,128)}, f32[3,128,128]{1,2,0:T(8,128)S(1)}, u32[]{:S(2)}) copy-start(f32[3,128,128]{1,2,0:T(8,128)S(1)} %custom-call.84) | copy-start | bytes 589828
  378.5 129.9 %copy-start.85 = (f32[128,1]{0,1:T(1,128)}, f32[128,1]{0,1:T(1,128)S(1)}, u32[]{:S(2)}) copy-start(f32[128,1]{0,1:T(1,128)S(1)} %convolution_bitcast_fusion.84) | copy-start | bytes 1540
  379.7 116.7 %copy-start.28 = (f32[128,384]{1,0:T(8,128)}, f32[128,384]{1,0:T(8,128)S(1)}, u32[]{:S(2)}) copy-start(f32[128,384]{1,0:T(8,128)S(1)} %fusion.203) | copy-start | bytes 589828
  454.3 45.9 %copy-start.20 = (f32[384,384]{1,0:T(8,128)}, f32[384,384]{1,0:T(8,128)S(1)}, u32[]{:S(2)}) copy-start(f32[384,384]{1,0:T(8,128)S(1)} %get-tuple-element.885) | copy-start | bytes 1769476
  507.3 10.5 collective-permute-start.2
  510.0 6.8 collective-permute-start.16
  517.4 132.6 %collective-permute-start.15 = (f32[384]{0:T(512)}, f32[384]{0:T(512)}, u32[]{:S(2)}, u32[]{:S(2)}) collective-permute-start(f32[384]{0:T(512)} %get-tuple-element.442), channel_id=1, source_target_pairs={{0,8},{8,16},{16,24},{24,32},{32,40},{40,48},{48,56},{56,64},{64,7... | collective-permute-start | bytes 4616 | tf_op jit(solution)/shard_map/ppermute | solution.py:11
  622.8 9.5 collective-permute-start.1
  630.1 19.9 %collective-permute-start.18 = (f32[384]{0:T(512)S(1)}, f32[384]{0:T(512)S(1)}, u32[]{:S(2)}, u32[]{:S(2)}) collective-permute-start(f32[384]{0:T(512)S(1)} %slice_subtract_fusion.34), channel_id=1, source_target_pairs={{0,16},{8,24},{16,32},{24,40},{32,48},{40,56},{48,64},{56,72},{64,... | collective-permute-start | bytes 4616 | tf_op jit(solution)/shard_map/ppermute | solution.py:11
  630.2 24.0 %collective-permute-start = (f32[384,384]{0,1:T(8,128)}, f32[384,384]{0,1:T(8,128)}, u32[]{:S(2)}, u32[]{:S(2)}) collective-permute-start(f32[384,384]{0,1:T(8,128)} %get-tuple-element.371), channel_id=1, source_target_pairs={{0,8},{8,16},{16,24},{24,32},{32,40},{40,48},{48,56},{56,64},{64,7... | collective-permute-start | bytes 1769480 | tf_op jit(solution)/shard_map/ppermute | solution.py:11
  643.6 19.8 %collective-permute-start.5 = (f32[384,384]{0,1:T(8,128)}, f32[384,384]{0,1:T(8,128)}, u32[]{:S(2)}, u32[]{:S(2)}) collective-permute-start(f32[384,384]{0,1:T(8,128)} %convolution_subtract_fusion.6), channel_id=1, source_target_pairs={{0,16},{8,24},{16,32},{24,40},{32,48},{40,56},{48,64},{56,72},{64,... | collective-permute-start | bytes 1769480 | tf_op jit(solution)/shard_map/ppermute | solution.py:11
  651.3 168.6 %collective-permute-start.17 = (f32[384]{0:T(512)}, f32[384]{0:T(512)}, u32[]{:S(2)}, u32[]{:S(2)}) collective-permute-start(f32[384]{0:T(512)} %get-tuple-element.344), channel_id=1, source_target_pairs={{0,16},{8,24},{16,32},{24,40},{32,48},{40,56},{48,64},{56,72},{64,... | collective-permute-start | bytes 4616 | tf_op jit(solution)/shard_map/ppermute | solution.py:11
  653.8 141.4 %collective-permute-start.4 = (f32[384,384]{1,0:T(8,128)}, f32[384,384]{1,0:T(8,128)S(1)}, u32[]{:S(2)}, u32[]{:S(2)}) collective-permute-start(f32[384,384]{1,0:T(8,128)} %copy.22), channel_id=1, source_target_pairs={{0,16},{8,24},{16,32},{24,40},{32,48},{40,56},{48,64},{56,72},{64,... | collective-permute-start | bytes 1769480 | tf_op jit(solution)/shard_map/ppermute | solution.py:11
  754.0 43.0 %copy-start.17 = (f32[384,384]{1,0:T(8,128)}, f32[384,384]{1,0:T(8,128)S(1)}, u32[]{:S(2)}) copy-start(f32[384,384]{1,0:T(8,128)S(1)} %get-tuple-element.881) | copy-start | bytes 1769476
  792.8 27.1 %collective-permute-start.20 = (f32[384]{0:T(512)S(1)}, f32[384]{0:T(512)S(1)}, u32[]{:S(2)}, u32[]{:S(2)}) collective-permute-start(f32[384]{0:T(512)S(1)} %sub.152), channel_id=1, source_target_pairs={{0,32},{8,40},{16,48},{24,56},{32,64},{40,72},{48,80},{56,88},{64,... | collective-permute-start | bytes 4616 | tf_op jit(solution)/shard_map/ppermute | solution.py:11
  809.6 164.9 %collective-permute-start.7 = (f32[384,384]{1,0:T(8,128)}, f32[384,384]{1,0:T(8,128)S(1)}, u32[]{:S(2)}, u32[]{:S(2)}) collective-permute-start(f32[384,384]{1,0:T(8,128)} %copy.26), channel_id=1, source_target_pairs={{0,32},{8,40},{16,48},{24,56},{32,64},{40,72},{48,80},{56,88},{64,... | collective-permute-start | bytes 1769480 | tf_op jit(solution)/shard_map/ppermute | solution.py:11
  812.2 22.4 %collective-permute-start.8 = (f32[384,384]{0,1:T(8,128)}, f32[384,384]{0,1:T(8,128)S(1)}, u32[]{:S(2)}, u32[]{:S(2)}) collective-permute-start(f32[384,384]{0,1:T(8,128)} %convolution_subtract_fusion.5), channel_id=1, source_target_pairs={{0,32},{8,40},{16,48},{24,56},{32,64},{40,72},{48,80},{56,88},{64,... | collective-permute-start | bytes 1769480 | tf_op jit(solution)/shard_map/ppermute | solution.py:11
  814.1 33.2 %collective-permute-start.3 = (f32[384,384]{0,1:T(8,128)}, f32[384,384]{0,1:T(8,128)S(1)}, u32[]{:S(2)}, u32[]{:S(2)}) collective-permute-start(f32[384,384]{0,1:T(8,128)} %get-tuple-element.455), channel_id=1, source_target_pairs={{0,16},{8,24},{16,32},{24,40},{32,48},{40,56},{48,64},{56,72},{64,... | collective-permute-start | bytes 1769480 | tf_op jit(solution)/shard_map/ppermute | solution.py:11
  821.1 171.5 %collective-permute-start.19 = (f32[384]{0:T(512)}, f32[384]{0:T(512)}, u32[]{:S(2)}, u32[]{:S(2)}) collective-permute-start(f32[384]{0:T(512)} %get-tuple-element.342), channel_id=1, source_target_pairs={{0,32},{8,40},{16,48},{24,56},{32,64},{40,72},{48,80},{56,88},{64,... | collective-permute-start | bytes 4616 | tf_op jit(solution)/shard_map/ppermute | solution.py:11
  972.8 19.9 %collective-permute-start.22 = (f32[384]{0:T(512)S(1)}, f32[384]{0:T(512)}, u32[]{:S(2)}, u32[]{:S(2)}) collective-permute-start(f32[384]{0:T(512)S(1)} %sub.154), channel_id=1, source_target_pairs={{0,64},{8,72},{16,80},{24,88},{32,96},{40,104},{48,112},{56,120},{... | collective-permute-start | bytes 4616 | tf_op jit(solution)/shard_map/ppermute | solution.py:11
  986.8 154.8 %collective-permute-start.10 = (f32[384,384]{1,0:T(8,128)}, f32[384,384]{1,0:T(8,128)S(1)}, u32[]{:S(2)}, u32[]{:S(2)}) collective-permute-start(f32[384,384]{1,0:T(8,128)} %copy.30), channel_id=1, source_target_pairs={{0,64},{8,72},{16,80},{24,88},{32,96},{40,104},{48,112},{56,120},{... | collective-permute-start | bytes 1769480 | tf_op jit(solution)/shard_map/ppermute | solution.py:11
  988.5 26.4 %collective-permute-start.11 = (f32[384,384]{0,1:T(8,128)}, f32[384,384]{0,1:T(8,128)S(1)}, u32[]{:S(2)}, u32[]{:S(2)}) collective-permute-start(f32[384,384]{0,1:T(8,128)} %convolution_subtract_fusion.4), channel_id=1, source_target_pairs={{0,64},{8,72},{16,80},{24,88},{32,96},{40,104},{48,112},{56,120},{... | collective-permute-start | bytes 1769480 | tf_op jit(solution)/shard_map/ppermute | solution.py:11
  988.7 26.2 %collective-permute-start.6 = (f32[384,384]{0,1:T(8,128)}, f32[384,384]{0,1:T(8,128)S(1)}, u32[]{:S(2)}, u32[]{:S(2)}) collective-permute-start(f32[384,384]{0,1:T(8,128)} %get-tuple-element.350), channel_id=1, source_target_pairs={{0,32},{8,40},{16,48},{24,56},{32,64},{40,72},{48,80},{56,88},{64,... | collective-permute-start | bytes 1769480 | tf_op jit(solution)/shard_map/ppermute | solution.py:11
  994.0 169.0 %collective-permute-start.21 = (f32[384]{0:T(512)}, f32[384]{0:T(512)}, u32[]{:S(2)}, u32[]{:S(2)}) collective-permute-start(f32[384]{0:T(512)} %get-tuple-element.340), channel_id=1, source_target_pairs={{0,64},{8,72},{16,80},{24,88},{32,96},{40,104},{48,112},{56,120},{... | collective-permute-start | bytes 4616 | tf_op jit(solution)/shard_map/ppermute | solution.py:11
  1101.6 41.9 %copy-start.18 = (f32[384,384]{1,0:T(8,128)}, f32[384,384]{1,0:T(8,128)S(1)}, u32[]{:S(2)}) copy-start(f32[384,384]{1,0:T(8,128)S(1)} %get-tuple-element.883) | copy-start | bytes 1769476
  1140.3 22.7 %collective-permute-start.24 = (f32[384]{0:T(512)S(1)}, f32[384]{0:T(512)S(1)}, u32[]{:S(2)}, u32[]{:S(2)}) collective-permute-start(f32[384]{0:T(512)S(1)} %sub.156), channel_id=1, source_target_pairs={{0,128},{8,136},{16,144},{24,152},{32,160},{40,168},{48,176},{56,1... | collective-permute-start | bytes 4616 | tf_op jit(solution)/shard_map/ppermute | solution.py:11
  1155.6 165.5 %collective-permute-start.13 = (f32[384,384]{1,0:T(8,128)}, f32[384,384]{1,0:T(8,128)S(1)}, u32[]{:S(2)}, u32[]{:S(2)}) collective-permute-start(f32[384,384]{1,0:T(8,128)} %copy.34), channel_id=1, source_target_pairs={{0,128},{8,136},{16,144},{24,152},{32,160},{40,168},{48,176},{56,1... | collective-permute-start | bytes 1769480 | tf_op jit(solution)/shard_map/ppermute | solution.py:11
  1158.3 27.9 %collective-permute-start.14 = (f32[384,384]{0,1:T(8,128)}, f32[384,384]{0,1:T(8,128)S(1)}, u32[]{:S(2)}, u32[]{:S(2)}) collective-permute-start(f32[384,384]{0,1:T(8,128)} %convolution_subtract_fusion.3), channel_id=1, source_target_pairs={{0,128},{8,136},{16,144},{24,152},{32,160},{40,168},{48,176},{56,1... | collective-permute-start | bytes 1769480 | tf_op jit(solution)/shard_map/ppermute | solution.py:11
  1159.1 36.3 %collective-permute-start.9 = (f32[384,384]{0,1:T(8,128)}, f32[384,384]{0,1:T(8,128)S(1)}, u32[]{:S(2)}, u32[]{:S(2)}) collective-permute-start(f32[384,384]{0,1:T(8,128)} %get-tuple-element.348), channel_id=1, source_target_pairs={{0,64},{8,72},{16,80},{24,88},{32,96},{40,104},{48,112},{56,120},{... | collective-permute-start | bytes 1769480 | tf_op jit(solution)/shard_map/ppermute | solution.py:11
  1164.2 170.0 %collective-permute-start.23 = (f32[384]{0:T(512)}, f32[384]{0:T(512)}, u32[]{:S(2)}, u32[]{:S(2)}) collective-permute-start(f32[384]{0:T(512)} %get-tuple-element.338), channel_id=1, source_target_pairs={{0,128},{8,136},{16,144},{24,152},{32,160},{40,168},{48,176},{56,1... | collective-permute-start | bytes 4616 | tf_op jit(solution)/shard_map/ppermute | solution.py:11
  1282.3 40.6 %copy-start.19 = (f32[384,384]{1,0:T(8,128)}, f32[384,384]{1,0:T(8,128)S(1)}, u32[]{:S(2)}) copy-start(f32[384,384]{1,0:T(8,128)S(1)} %get-tuple-element.884) | copy-start | bytes 1769476
  1329.3 17.4 %collective-permute-start.12 = (f32[384,384]{0,1:T(8,128)}, f32[384,384]{0,1:T(8,128)}, u32[]{:S(2)}, u32[]{:S(2)}) collective-permute-start(f32[384,384]{0,1:T(8,128)} %get-tuple-element.346), channel_id=1, source_target_pairs={{0,128},{8,136},{16,144},{24,152},{32,160},{40,168},{48,176},{56,1... | collective-permute-start | bytes 1769480 | tf_op jit(solution)/shard_map/ppermute | solution.py:11
  1412.6 44.6 %copy-start.88 = (f32[128,1]{0,1:T(1,128)S(1)}, f32[128,1]{0,1:T(1,128)}, u32[]{:S(2)}) copy-start(f32[128,1]{0,1:T(1,128)} %copy-done.87) | copy-start | bytes 1540
  1412.6 44.6 %copy-start.106 = (f32[128,1]{0,1:T(1,128)S(1)}, f32[128,1]{0,1:T(1,128)}, u32[]{:S(2)}) copy-start(f32[128,1]{0,1:T(1,128)} %copy-done.105) | copy-start | bytes 1540
  1412.6 44.6 %copy-start.121 = (f32[128,1]{0,1:T(1,128)S(1)}, f32[128,1]{0,1:T(1,128)}, u32[]{:S(2)}) copy-start(f32[128,1]{0,1:T(1,128)} %copy-done.120) | copy-start | bytes 1540
  1412.6 44.6 %copy-start.84 = (f32[128,1]{0,1:T(1,128)S(1)}, f32[128,1]{0,1:T(1,128)}, u32[]{:S(2)}) copy-start(f32[128,1]{0,1:T(1,128)} %copy-done.83) | copy-start | bytes 1540
  1412.7 44.6 %copy-start.86 = (f32[128,1]{0,1:T(1,128)S(1)}, f32[128,1]{0,1:T(1,128)}, u32[]{:S(2)}) copy-start(f32[128,1]{0,1:T(1,128)} %copy-done.85) | copy-start | bytes 1540
  1412.7 44.6 %copy-start.101 = (f32[128,1]{0,1:T(1,128)S(1)}, f32[128,1]{0,1:T(1,128)}, u32[]{:S(2)}) copy-start(f32[128,1]{0,1:T(1,128)} %copy-done.99) | copy-start | bytes 1540
  1412.7 44.6 %copy-start.104 = (f32[128,1]{0,1:T(1,128)S(1)}, f32[128,1]{0,1:T(1,128)}, u32[]{:S(2)}) copy-start(f32[128,1]{0,1:T(1,128)} %copy-done.102) | copy-start | bytes 1540
  1412.7 44.6 %copy-start.116 = (f32[128,1]{0,1:T(1,128)S(1)}, f32[128,1]{0,1:T(1,128)}, u32[]{:S(2)}) copy-start(f32[128,1]{0,1:T(1,128)} %copy-done.114) | copy-start | bytes 1540
  1412.7 44.6 %copy-start.119 = (f32[128,1]{0,1:T(1,128)S(1)}, f32[128,1]{0,1:T(1,128)}, u32[]{:S(2)}) copy-start(f32[128,1]{0,1:T(1,128)} %copy-done.117) | copy-start | bytes 1540
  1412.7 47.5 %copy-start.22 = (f32[128,768]{1,0:T(8,128)S(1)}, f32[128,768]{1,0:T(8,128)}, u32[]{:S(2)}) copy-start(f32[128,768]{1,0:T(8,128)} %copy-done.21) | copy-start | bytes 1179652
  1421.7 40.8 %copy-start.24 = (f32[128,768]{1,0:T(8,128)S(1)}, f32[128,768]{1,0:T(8,128)}, u32[]{:S(2)}) copy-start(f32[128,768]{1,0:T(8,128)} %copy-done.23) | copy-start | bytes 1179652
  1457.2 3.0 collective-permute-start.25
  (104 other events, 597.8 us)
Sparse Core Ops, SparseCore 0:
  28.4 133.5 all-reduce.11
where the time goes:
time: 1510 us; the launch traced here: 1480 us
  other arithmetic  841 us (56%)
  matrix products  225 us (15%)
  waiting for transfers between devices  193 us (13%)
  local copies, waits for them, and re-layouts  112 us (7%)
  starting transfers between devices  43.2 us (3%)
  blocking collectives  34.4 us (2%)
  between operations  34.2 us (2%)
    another operation x55, other arithmetic, merge(): chol = jnp.linalg.cholesky(arr_a + bll)  314 us
    another operation x32, other arithmetic, segment_complement(): chol = jnp.linalg.cholesky(block)  171 us
    another operation x15, other arithmetic, merge(): weights = jax.scipy.linalg.cho_solve((chol, True), couple)  158 us
    psum x1, waiting for transfers between devices, shards(): diag, off, grad = lax.psum((diag_part, off_part, grad_part), 'band')  96.8 us
    ppermute x26, waiting for transfers between devices, shifted_2(): lax.ppermute(shard, axis, [(i, (i + by) % devices) for i in range(devices)])  95.9 us
    another operation x9, other arithmetic, lower_solve(): return jax.scipy.linalg.solve_triangular(chol, rhs, lower=True)  89.3 us
    dot_general x42, matrix products, matmul_high(): return jnp.matmul(left, right, precision=HIGH)  74.9 us
    another operation x11, other arithmetic, closure(): chol = jnp.linalg.cholesky(whole)  57 us
  transfers between devices with their start and end apart: 27, of which 11 were waited for; matrix products, arithmetic and copies ran while one was open for 46% of the time, Pallas kernels for 0%

commit v1 on v0

v1 whole, which is shorter than its diff:
```python
import functools
import jax
import jax.numpy as jnp
from jax import lax
from jax.experimental import pallas as pl
from jax.experimental.pallas import tpu as pltpu
from jax.sharding import PartitionSpec as P

HIGH = lax.Precision.HIGHEST
B = 128
f32 = jnp.float32
VMEM = pl.BlockSpec(memory_space=pltpu.VMEM)
PARAMS = pltpu.CompilerParams(vmem_limit_bytes=48 << 20)


def dg(a, b, ca, cb):
    return lax.dot_general(a, b, (((ca,), (cb,)), ((), ())), precision=HIGH, preferred_element_type=f32)


def nn(a, b):
    return dg(a, b, 1, 0)


def nt(a, b):
    return dg(a, b, 1, 1)


def tn(a, b):
    return dg(a, b, 0, 0)


def iota2(shape):
    return lax.broadcasted_iota(jnp.int32, shape, 0), lax.broadcasted_iota(jnp.int32, shape, 1)


def inverse_factors(mats):
    mats = [[m[8 * i : 8 * i + 8, :] for i in range(B // 8)] for m in mats]
    sub, lane = iota2((8, B))
    wide = lambda x: jnp.broadcast_to(x, (8, B))
    for p in range(B // 8):
        k = 8 * p
        panel = (lane >= k) & (lane < k + 8)
        eye = jnp.where(lane == sub + k, 1.0, 0.0)
        state = []
        for m in mats:
            cols = [wide(m[p][:, k + j : k + j + 1]) for j in range(8)]
            g = {(i, j): wide(cols[j][i : i + 1, :]) for j in range(8) for i in range(j, 8)}
            start = jnp.where(panel, eye, m[p])
            r = [wide(start[j : j + 1, :]) for j in range(8)]
            state.append((g, r, [None] * 8, {}))
        for j in range(8):
            for g, r, inv, l in state:
                inv[j] = 1.0 / g[j, j]
            for g, r, inv, l in state:
                for i in range(j + 1, 8):
                    l[i, j] = g[i, j] * inv[j]
                for i in range(j + 1, 8):
                    for h in range(i, 8):
                        g[h, i] = g[h, i] - l[h, j] * g[i, j]
                for i in range(j + 1, 8):
                    r[i] = r[i] - l[i, j] * r[j]
        solved = []
        for g, r, inv, l in state:
            y = [None] * 8
            for j in range(7, -1, -1):
                acc = r[j] * inv[j]
                for i in range(7, j, -1):
                    acc = acc - l[i, j] * y[i]
                y[j] = acc
            solved.append(y)
        for i in range(p + 1, B // 8):
            for m, y in zip(mats, solved):
                c = [wide(m[i][:, k + j : k + j + 1]) for j in range(8)]
                even = c[0] * y[0]
                odd = c[1] * y[1]
                for j in range(2, 8, 2):
                    even = even + c[j] * y[j]
                    odd = odd + c[j + 1] * y[j + 1]
                m[i] = jnp.where(panel, 0.0, m[i]) - (even + odd)
        for m, (g, r, inv, l) in zip(mats, state):
            out = r[0] * lax.rsqrt(g[0, 0])
            for j in range(1, 8):
                out = jnp.where(sub == j, r[j] * lax.rsqrt(g[j, j]), out)
            m[p] = jnp.where(lane < k + 8, out, 0.0)
    return [jnp.concatenate(m, axis=0) for m in mats]


def factor(blocks, stores):
    n = range(len(blocks))
    zero = jnp.zeros((B, B), f32)
    x11 = inverse_factors([blocks[q](0, 0) for q in n])
    w21 = [nt(blocks[q](1, 0), x11[q]) for q in n]
    w31 = [nt(blocks[q](2, 0), x11[q]) for q in n]
    s22 = [blocks[q](1, 1) - nt(w21[q], w21[q]) for q in n]
    s32 = [blocks[q](2, 1) - nt(w31[q], w21[q]) for q in n]
    s33 = [blocks[q](2, 2) - nt(w31[q], w31[q]) for q in n]
    x22 = inverse_factors(s22)
    w32 = [nt(s32[q], x22[q]) for q in n]
    s33 = [s33[q] - nt(w32[q], w32[q]) for q in n]
    x21 = [-nn(x22[q], nn(w21[q], x11[q])) for q in n]
    x33 = inverse_factors(s33)
    for q in n:
        x31 = -nn(x33[q], nn(w31[q], x11[q]) + nn(w32[q], x21[q]))
        x32 = -nn(x33[q], nn(w32[q], x22[q]))
        stores[q][0:B, :] = jnp.concatenate([x11[q], zero, zero], axis=1)
        stores[q][B : 2 * B, :] = jnp.concatenate([x21[q], x22[q], zero], axis=1)
        stores[q][2 * B :, :] = jnp.concatenate([x31, x32, x33[q]], axis=1)


def block(ref, i, j):
    return ref[B * i : B * i + B, B * j : B * j + B]


def diagonal(row):
    r, c = iota2((B, B))
    return jnp.where(r == c, jnp.broadcast_to(row, (B, B)), 0.0)


def lower_of(tri, i, j):
    if i > j:
        return block(tri, i, j)
    r, c = iota2((B, B))
    t = block(tri, i, i)
    return jnp.where(r >= c, t, t.T)


def upper_of(tri, diag, i, j):
    if i > j:
        return block(tri, j, i).T
    r, c = iota2((B, B))
    t = jnp.where(r < c, block(tri, i, i), 0.0)
    return t + t.T + diagonal(diag[:, B * i : B * i + B])


def reduce_arc(x, left_cross, right_cross, rhs, left, right, left_rhs, right_rhs, tri_out, cross_out, vec_out):
    n = x.shape[0]
    nb = n // B
    va = nt(left_cross, x)
    ub = nn(x, right_cross)
    u = nt(rhs, x)
    r, c = iota2((B, B))
    cut = lambda m, i: m[B * i : B * i + B, :]
    col = lambda m, i: m[:, B * i : B * i + B]
    diags = []
    for i in range(nb):
        for j in range(i):
            tri_out[B * i : B * i + B, B * j : B * j + B] = left(i, j) - nt(cut(va, i), cut(va, j))
        ll = left(i, i) - nt(cut(va, i), cut(va, i))
        rr = right(i, i) - tn(col(ub, i), col(ub, i))
        tri_out[B * i : B * i + B, B * i : B * i + B] = jnp.where(r >= c, ll, rr)
        diags.append(jnp.sum(jnp.where(r == c, rr, 0.0), axis=0, keepdims=True))
        for j in range(i + 1, nb):
            tri_out[B * i : B * i + B, B * j : B * j + B] = right(i, j) - tn(col(ub, i), col(ub, j))
    cross_out[...] = -nn(va, ub)
    new_l = left_rhs - nt(u, va)[0:1]
    new_r = right_rhs - nn(u, ub)[0:1]
    pad = jnp.zeros((5, n), f32)
    vec_out[...] = jnp.concatenate([new_l, new_r, jnp.concatenate(diags, axis=1), pad], axis=0)
    return va, ub, u


def gram_kernel(first_ref, second_ref, resid_ref, out_ref):
    links = first_ref.shape[0]
    size = first_ref.shape[2]
    dot = lambda a, b: jnp.dot(a, b, preferred_element_type=f32)
    r, c = iota2((size, size))
    diag = [None] * (links + 1)
    grad = [None] * (links + 1)
    plus = lambda x, y: y if x is None else x + y
    resid = resid_ref[...].astype(f32)
    for i in range(links):
        a = first_ref[i]
        b = second_ref[i]
        at = a.T
        bt = b.T
        e = jnp.broadcast_to(resid[i : i + 1, :], (8, resid.shape[1])).astype(jnp.bfloat16)
        paa = dot(at, a)
        pab = dot(at, b)
        ga = dot(e, a)[0:1]
        diag[i] = plus(diag[i], paa)
        diag[i + 1] = dot(bt, b) - pab - dot(bt, a) + paa
        grad[i] = plus(grad[i], ga)
        grad[i + 1] = dot(e, b)[0:1] - ga
        out_ref[(3 + i) * size : (4 + i) * size, :] = pab - paa
    out_ref[0:size, :] = jnp.where(r >= c, diag[1], diag[3])
    out_ref[2 * size : 3 * size, :] = diag[2]
    d3 = jnp.sum(jnp.where(r == c, diag[3], 0.0), axis=0, keepdims=True)
    out_ref[size : 2 * size, :] = jnp.where(r >= c, diag[0], diag[4])
    d4 = jnp.sum(jnp.where(r == c, diag[4], 0.0), axis=0, keepdims=True)
    rows = [-g for g in grad] + [d3, d4, jnp.zeros((1, size), f32)]
    out_ref[7 * size : 7 * size + 8, :] = jnp.concatenate(rows, axis=0)


def segment_kernel(sums, damp_inner, damp_sep, tri_out, cross_out, vec_out, x_out, va_out, ub_out, u_out, tri_s, cross_s, vec_s):
    size = tri_out.shape[0]
    part = lambda k: sums.at[k * size : (k + 1) * size, :]
    inner, ends, mid = part(0), part(1), part(2)
    cross = [part(3 + k) for k in range(4)]
    row = lambda k: sums[7 * size + k : 7 * size + k + 1, :]
    damp = lambda k, i: diagonal(damp_inner[k : k + 1, B * i : B * i + B])

    def first(i, j):
        s = lower_of(inner, i, j)
        return s + damp(0, i) if i == j else s

    def third(i, j):
        s = upper_of(inner, row(5), i, j)
        return s + damp(2, i) if i == j else s

    factor([first, third], [x_out.at[0], x_out.at[1]])
    zero = jnp.zeros((B, B), f32)
    wide = lambda v: jnp.broadcast_to(v, (8, size))
    none = lambda i, j: zero
    zrow = jnp.zeros((1, size), f32)

    def end(i, j):
        if i < j:
            return block(ends, i, j)
        t = upper_of(ends, row(6), i, i)
        return t + diagonal(damp_sep[:, B * i : B * i + B])

    out = reduce_arc(x_out[0], cross[0][...], cross[1][...], wide(row(1)), lambda i, j: lower_of(ends, i, j), none,
                     row(0), zrow, tri_s.at[0], cross_s.at[0], vec_s.at[0])
    va_out[0], ub_out[0], u_out[0] = out
    out = reduce_arc(x_out[1], cross[2][...], cross[3][...], wide(row(3)), lambda i, j: block(mid, i, j), end,
                     zrow, row(4), tri_s.at[1], cross_s.at[1], vec_s.at[1])
    va_out[1], ub_out[1], u_out[1] = out

    def second(i, j):
        s = upper_of(tri_s.at[0], vec_s[0][2:3], i, j) + lower_of(tri_s.at[1], i, j)
        return s + damp(1, i) if i == j else s

    factor([second], [x_out.at[2]])
    rhs = wide(row(2) + vec_s[0][1:2] + vec_s[1][0:1])
    out = reduce_arc(x_out[2], cross_s[0], cross_s[1], rhs, lambda i, j: lower_of(tri_s.at[0], i, j),
                     lambda i, j: upper_of(tri_s.at[1], vec_s[1][2:3], i, j) if i == j else block(tri_s.at[1], i, j),
                     vec_s[0][0:1], vec_s[1][1:2], tri_out, cross_out, vec_out)
    va_out[2], ub_out[2], u_out[2] = out


def merge_kernel(tri_a, cross_a, vec_a, tri_b, cross_b, vec_b, tri_out, cross_out, vec_out, x):
    size = tri_out.shape[0]

    def shared(i, j):
        return upper_of(tri_a, vec_a[2:3], i, j) + lower_of(tri_b, i, j)

    factor([shared], [x])
    rhs = jnp.broadcast_to(vec_a[1:2] + vec_b[0:1], (8, size))
    reduce_arc(x[...], cross_a[...], cross_b[...], rhs, lambda i, j: lower_of(tri_a, i, j),
               lambda i, j: upper_of(tri_b, vec_b[2:3], i, j) if i == j else block(tri_b, i, j),
               vec_a[0:1], vec_b[1:2], tri_out, cross_out, vec_out)


def closure_kernel(tri, cross, vec, top, x):
    size = tri.shape[0]

    def whole(i, j):
        return (lower_of(tri, i, j) + upper_of(tri, vec[2:3], i, j)) + (block(cross, i, j) + block(cross, j, i).T)

    factor([whole], [x])
    rhs = jnp.broadcast_to(vec[0:1] + vec[1:2], (8, size))
    top[...] = nn(nt(rhs, x[...]), x[...])


def interior_kernel(left, right, x, va, ub, u, out):
    def middle(q, l, r):
        return nn(u[q] - nn(l, va[q]) - nt(r, ub[q]), x[q])

    second = middle(2, left[...], right[...])
    first = middle(0, left[...], second)
    third = middle(1, second, right[...])
    out[...] = jnp.concatenate([first[0:1], second[0:1], third[0:1], jnp.zeros((5, first.shape[1]), f32)], axis=0)


def call(kernel, outs, args, name, scratch=()):
    return pl.pallas_call(
        kernel, out_shape=[jax.ShapeDtypeStruct(s, f32) for s in outs], in_specs=[VMEM] * len(args),
        out_specs=[VMEM] * len(outs), scratch_shapes=[pltpu.VMEM(s, f32) for s in scratch],
        compiler_params=PARAMS, name=name)(*args)


def shift(arrays, by):
    count = lax.axis_size("seg")
    return [lax.ppermute(a, "seg", [(i, (i + by) % count) for i in range(count)]) for a in arrays]


def shards(jac_first, jac_second, residual, damp_inner, damp_sep):
    size = jac_first.shape[-1]
    square, rows = (size, size), (8, size)
    arc_shapes = [square, square, rows]
    (part,) = call(gram_kernel, [(7 * size + 8, size)], (jac_first[0], jac_second[0], residual[0]), "gram")
    sums = lax.psum(part, "band")
    *arc, x, va, ub, u = call(
        segment_kernel, arc_shapes + [(3, *square)] * 3 + [(3, *rows)], (sums, damp_inner[0], damp_sep), "segment",
        [(2, *square), (2, *square), (2, *rows)])
    levels = lax.axis_size("seg").bit_length() - 1
    for level in range(levels):
        other = shift(arc, 1 << level)
        arc = call(merge_kernel, arc_shapes, (*other, *arc), "merge", [square])
    (top,) = call(closure_kernel, [rows], arc, "closure", [square])
    (left,) = shift([top], 1)
    (inner,) = call(interior_kernel, [rows], (left, top, x, va, ub, u), "interior")
    return (top[0:1], inner[None, 0:3])


def solution(mesh):
    return jax.shard_map(
        shards,
        mesh=mesh,
        in_specs=(
            P("seg", None, "band", None),
            P("seg", None, "band", None),
            P("seg", None, "band"),
            P("seg", None, None),
            P("seg", None),
        ),
        out_specs=(P("seg", None), P("seg", None, None)),
        check_vma=False,
    )
```

time: 1510 us -> 478 us (0.32); the launches traced: 1480 us -> 469 us
  other arithmetic: 841 us -> 0 us
  matrix products: 225 us -> 0 us
  Pallas kernels: 0 us -> 213 us
  local copies, waits for them, and re-layouts: 112 us -> 5.36 us
  blocking collectives: 34.4 us -> 0 us
  between operations: 34.2 us -> 14.2 us
  waiting for transfers between devices: 193 us -> 212 us
  starting transfers between devices: 43.2 us -> 24.4 us
    another operation x129 -> x0, other arithmetic: 820 us -> none  [the longest x55 314 us: merge(): chol = jnp.linalg.cholesky(arr_a + bll)]
    pallas_call x0 -> x9, Pallas kernels: none -> 213 us  [call(): pl.pallas_call(kernel, out_shape=[jax.ShapeDtypeStruct(s, f32) for s in o...]
    another operation x201 -> x0, matrix products: 138 us -> none  [the longest x50 37.8 us: merge(): weights = jax.scipy.linalg.cho_solve((chol, True), couple)]
    dot_general x47 -> x0, matrix products: 87 us -> none  [the longest x42 74.9 us: matmul_high(): return jnp.matmul(left, right, precision=HIGH)]
    another operation x118 -> x0, local copies, waits for them, and re-layouts: 71.9 us -> none  [the longest x45 36.2 us: merge(): weights = jax.scipy.linalg.cho_solve((chol, True), couple)]
    psum x1 -> x0, blocking collectives: 34.4 us -> none  [shards(): diag, off, grad = lax.psum((diag_part, off_part, grad_part), 'band')]
    ppermute x26 -> x16, starting transfers between devices: 43.1 us -> 24.4 us  [shift(): lax.ppermute(a, 'seg', [(i, (i + by) % count) for i in range(count)])]
    ppermute x26 -> x16, waiting for transfers between devices: 95.9 us -> 102 us  [shift(): lax.ppermute(a, 'seg', [(i, (i + by) % count) for i in range(count)])]
  transfers between devices with their start and end apart: 27 -> 17, of which waited for: 11 -> 7; matrix products, arithmetic and copies ran while one was open for 46% -> 0% of each run, Pallas kernels for 0% -> 0%
where the time goes in v1:
time: 478 us; the launch traced here: 469 us
  Pallas kernels  213 us (45%)
  waiting for transfers between devices  212 us (44%)
  starting transfers between devices  24.4 us (5%)
  between operations  14.2 us (3%)
  local copies, waits for them, and re-layouts  5.36 us (1%)
    pallas_call x9, Pallas kernels, call(): pl.pallas_call(kernel, out_shape=[jax.ShapeDtypeStruct(s, f32) for s in o...  213 us
    psum x1, waiting for transfers between devices, shards(): sums = lax.psum(part, 'band')  111 us
    ppermute x16, waiting for transfers between devices, shift(): lax.ppermute(a, 'seg', [(i, (i + by) % count) for i in range(count)])  102 us
    ppermute x16, starting transfers between devices, shift(): lax.ppermute(a, 'seg', [(i, (i + by) % count) for i in range(count)])  24.4 us
  transfers between devices with their start and end apart: 17, of which 7 were waited for; matrix products, arithmetic and copies ran while one was open for 0% of the time, Pallas kernels for 0%

profile of v1, /device:TPU:6, one launch (start us, length us, event | category | flops | bytes accessed | tf_op | source)
XLA Modules:
  0.0 469.3 jit_solution(5083949805016884608)
XLA Ops:
  7.2 0.0 all-reduce.2.cloned.1.call-start
  7.2 1.4 copy-done.1
  8.6 1.4 copy-done.2
  10.0 0.7 copy-done.3
  10.7 6.1 %gram.1 = f32[2696,384]{1,0:T(8,128)} custom-call(bf16[4,512,384]{2,1,0:T(8,128)(2,1)S(1)} %bitcast.8, bf16[4,512,384]{2,1,0:T(8,128)(2,1)S(1)} %bitcast.9, bf16[4,512]{1,0:T(4,128)(2,1)S(1)} %bitcast.11), custom_call_target="tpu_custom_call" | custom-call | tf_op jit(solution)/shard_map/gram/pallas_call | solution.py:276
  16.8 0.0 all-reduce.2.cloned.1.call-update
  16.9 0.7 copy-done.5
  17.5 110.8 %all-reduce.2.cloned.1.call-done.sums = f32[2696,384]{1,0:T(8,128)} async-done(((f32[2696,384]{1,0:T(8,128)}), f32[2696,384]{1,0:T(8,128)}) %all-reduce.2.cloned.1.call-update) | async-done | bytes 4141072 | tf_op jit(solution)/shard_map/psum | solution.py:292
  128.3 65.3 %segment.1 = (f32[384,384]{1,0:T(8,128)S(1)}, f32[384,384]{1,0:T(8,128)S(1)}, f32[8,384]{1,0:T(8,128)S(1)}, f32[3,384,384]{2,1,0:T(8,128)S(1)}, f32[3,384,384]{2...) custom-call(f32[2696,384]{1,0:T(8,128)} %all-reduce.2.cloned.1.call-done.sums, ...), custom_call_target="tpu_custom_call" | custom-call | tf_op jit(solution)/shard_map/segment/pallas_call | solution.py:276
  193.7 0.0 collective-permute-start
  193.7 1.6 collective-permute-start.1
  195.3 0.0 collective-permute-start.2
  195.3 14.1 %collective-permute-done.2.vec_a = f32[8,384]{1,0:T(8,128)S(1)} collective-permute-done((f32[8,384]{1,0:T(8,128)S(1)}, f32[8,384]{1,0:T(8,128)S(1)}, u32[]{:S(2)}, u32[]{:S(2)}) %collective-permute-start.2) | collective-permute-done | bytes 12320 | tf_op jit(solution)/shard_map/ppermute | solution.py:284
  209.4 0.0 collective-permute-done.tri_a
  209.4 0.0 collective-permute-done.1.cross_a
  209.4 24.1 %merge.5 = (f32[384,384]{1,0:T(8,128)S(1)}, f32[384,384]{1,0:T(8,128)S(1)}, f32[8,384]{1,0:T(8,128)S(1)}) custom-call(f32[384,384]{1,0:T(8,128)S(1)} %collective-permute-done.tri_a, f32[384,384]{1,0:T(8,128)S(1)} %collective-permute-done.1.cross_a, f32[8,384]{1,0:T(8,128)S(1)} %collective-permute-done.2.vec_a, f32[384,384]{1,0:T(8,128)S(1)} %get-tuple-element.24.tri_b, ...), custom_call_target="tpu_custom_call" | custom-call | tf_op jit(solution)/shard_map/merge/pallas_call | solution.py:276
  233.5 3.6 collective-permute-start.3
  237.1 0.1 collective-permute-start.4
  237.2 2.8 collective-permute-start.5
  240.0 20.8 %collective-permute-done.5.vec_a = f32[8,384]{1,0:T(8,128)S(1)} collective-permute-done((f32[8,384]{1,0:T(8,128)S(1)}, f32[8,384]{1,0:T(8,128)S(1)}, u32[]{:S(2)}, u32[]{:S(2)}) %collective-permute-start.5) | collective-permute-done | bytes 12320 | tf_op jit(solution)/shard_map/ppermute | solution.py:284
  260.8 0.0 collective-permute-done.3.tri_a
  260.8 0.0 collective-permute-done.4.cross_a
  260.8 23.9 %merge.6 = (f32[384,384]{1,0:T(8,128)S(1)}, f32[384,384]{1,0:T(8,128)S(1)}, f32[8,384]{1,0:T(8,128)S(1)}) custom-call(f32[384,384]{1,0:T(8,128)S(1)} %collective-permute-done.3.tri_a, f32[384,384]{1,0:T(8,128)S(1)} %collective-permute-done.4.cross_a, f32[8,384]{1,0:T(8,128)S(1)} %collective-permute-done.5.vec_a, f32[384,384]{1,0:T(8,128)S(1)} %get-tuple-element.27.tri_b, ...), custom_call_target="tpu_custom_call" | custom-call | tf_op jit(solution)/shard_map/merge/pallas_call | solution.py:276
  284.7 2.4 collective-permute-start.6
  287.0 2.1 collective-permute-start.7
  289.1 2.7 collective-permute-start.8
  291.9 20.6 %collective-permute-done.8.vec_a = f32[8,384]{1,0:T(8,128)S(1)} collective-permute-done((f32[8,384]{1,0:T(8,128)S(1)}, f32[8,384]{1,0:T(8,128)S(1)}, u32[]{:S(2)}, u32[]{:S(2)}) %collective-permute-start.8) | collective-permute-done | bytes 12320 | tf_op jit(solution)/shard_map/ppermute | solution.py:284
  312.5 0.0 collective-permute-done.6.tri_a
  312.5 0.0 collective-permute-done.7.cross_a
  312.5 23.9 %merge.7 = (f32[384,384]{1,0:T(8,128)S(1)}, f32[384,384]{1,0:T(8,128)S(1)}, f32[8,384]{1,0:T(8,128)S(1)}) custom-call(f32[384,384]{1,0:T(8,128)S(1)} %collective-permute-done.6.tri_a, f32[384,384]{1,0:T(8,128)S(1)} %collective-permute-done.7.cross_a, f32[8,384]{1,0:T(8,128)S(1)} %collective-permute-done.8.vec_a, f32[384,384]{1,0:T(8,128)S(1)} %get-tuple-element.30.tri_b, ...), custom_call_target="tpu_custom_call" | custom-call | tf_op jit(solution)/shard_map/merge/pallas_call | solution.py:276
  336.4 1.5 collective-permute-start.9
  337.9 0.9 collective-permute-start.10
  338.7 2.2 collective-permute-start.11
  341.0 22.0 %collective-permute-done.11.vec_a = f32[8,384]{1,0:T(8,128)S(1)} collective-permute-done((f32[8,384]{1,0:T(8,128)S(1)}, f32[8,384]{1,0:T(8,128)S(1)}, u32[]{:S(2)}, u32[]{:S(2)}) %collective-permute-start.11) | collective-permute-done | bytes 12320 | tf_op jit(solution)/shard_map/ppermute | solution.py:284
  363.0 23.9 %merge.8 = (f32[384,384]{1,0:T(8,128)S(1)}, f32[384,384]{1,0:T(8,128)S(1)}, f32[8,384]{1,0:T(8,128)S(1)}) custom-call(f32[384,384]{1,0:T(8,128)S(1)} %collective-permute-done.9.tri_a, f32[384,384]{1,0:T(8,128)S(1)} %collective-permute-done.10.cross_a, f32[8,384]{1,0:T(8,128)S(1)} %collective-permute-done.11.vec_a, f32[384,384]{1,0:T(8,128)S(1)} %get-tuple-element.33.tri_b, ...), custom_call_target="tpu_custom_call" | custom-call | tf_op jit(solution)/shard_map/merge/pallas_call | solution.py:276
  386.9 0.9 collective-permute-start.12
  387.8 2.6 collective-permute-start.13
  390.4 0.9 collective-permute-start.14
  391.3 21.5 %collective-permute-done.14.vec_a = f32[8,384]{1,0:T(8,128)S(1)} collective-permute-done((f32[8,384]{1,0:T(8,128)S(1)}, f32[8,384]{1,0:T(8,128)S(1)}, u32[]{:S(2)}, u32[]{:S(2)}) %collective-permute-start.14) | collective-permute-done | bytes 12320 | tf_op jit(solution)/shard_map/ppermute | solution.py:284
  412.8 0.0 collective-permute-done.12.tri_a
  412.8 0.0 collective-permute-done.13.cross_a
  412.8 24.1 %merge.9 = (f32[384,384]{1,0:T(8,128)S(1)}, f32[384,384]{1,0:T(8,128)S(1)}, f32[8,384]{1,0:T(8,128)S(1)}) custom-call(f32[384,384]{1,0:T(8,128)S(1)} %collective-permute-done.12.tri_a, f32[384,384]{1,0:T(8,128)S(1)} %collective-permute-done.13.cross_a, f32[8,384]{1,0:T(8,128)S(1)} %collective-permute-done.14.vec_a, f32[384,384]{1,0:T(8,128)S(1)} %get-tuple-element.36.tri_b, ...), custom_call_target="tpu_custom_call" | custom-call | tf_op jit(solution)/shard_map/merge/pallas_call | solution.py:276
  436.9 18.0 %closure.1.right = f32[8,384]{1,0:T(8,128)S(1)} custom-call(f32[384,384]{1,0:T(8,128)S(1)} %get-tuple-element.39.tri, f32[384,384]{1,0:T(8,128)S(1)} %get-tuple-element.40.cross, f32[8,384]{1,0:T(8,128)S(1)} %get-tuple-element.41.vec), custom_call_target="tpu_custom_call" | custom-call | tf_op jit(solution)/shard_map/closure/pallas_call | solution.py:276
  454.9 0.0 collective-permute-start.15
  454.9 0.6 slice.8
  455.5 2.6 collective-permute-done.15.left
  458.1 3.6 interior.1
  461.7 0.6 copy.7
  (12 shorter events, 0.0 us)
Async XLA Ops:
  7.2 121.2 %all-reduce.2.cloned.1.call-start = ((), (), s32[]{:S(2)}) async-start(), calls=%async_computation | async-start | bytes 8282112 | tf_op jit(solution)/shard_map/psum | solution.py:292
  7.2 1.4 copy-start.1
  8.6 1.4 copy-start.2
  10.0 0.7 copy-start.3
  16.8 0.7 copy-start.5
  16.8 111.5 %copy-start.4 = (f32[1,384]{1,0:T(1,128)S(1)}, f32[1,384]{1,0:T(1,128)}, u32[]{:S(2)}) copy-start(f32[1,384]{1,0:T(1,128)} %damp_sep.1) | copy-start | bytes 4612
  193.7 15.8 %collective-permute-start = (f32[384,384]{1,0:T(8,128)S(1)}, f32[384,384]{1,0:T(8,128)S(1)}, u32[]{:S(2)}, u32[]{:S(2)}) collective-permute-start(f32[384,384]{1,0:T(8,128)S(1)} %get-tuple-element.24.tri_b), channel_id=1, source_target_pairs={{0,8},{8,16},{16,24},{24,32},{32,40},{40,48},{48,56},{56,64},{64,7... | collective-permute-start | bytes 1769480 | tf_op jit(solution)/shard_map/ppermute | solution.py:284
  193.7 15.8 %collective-permute-start.1 = (f32[384,384]{1,0:T(8,128)S(1)}, f32[384,384]{1,0:T(8,128)S(1)}, u32[]{:S(2)}, u32[]{:S(2)}) collective-permute-start(f32[384,384]{1,0:T(8,128)S(1)} %get-tuple-element.25.cross_b), channel_id=1, source_target_pairs={{0,8},{8,16},{16,24},{24,32},{32,40},{40,48},{48,56},{56,64},{64,7... | collective-permute-start | bytes 1769480 | tf_op jit(solution)/shard_map/ppermute | solution.py:284
  195.3 14.2 %collective-permute-start.2 = (f32[8,384]{1,0:T(8,128)S(1)}, f32[8,384]{1,0:T(8,128)S(1)}, u32[]{:S(2)}, u32[]{:S(2)}) collective-permute-start(f32[8,384]{1,0:T(8,128)S(1)} %get-tuple-element.26.vec_b), channel_id=1, source_target_pairs={{0,8},{8,16},{16,24},{24,32},{32,40},{40,48},{48,56},{56,64},{64,7... | collective-permute-start | bytes 36872 | tf_op jit(solution)/shard_map/ppermute | solution.py:284
  233.5 27.3 %collective-permute-start.3 = (f32[384,384]{1,0:T(8,128)S(1)}, f32[384,384]{1,0:T(8,128)S(1)}, u32[]{:S(2)}, u32[]{:S(2)}) collective-permute-start(f32[384,384]{1,0:T(8,128)S(1)} %get-tuple-element.27.tri_b), channel_id=1, source_target_pairs={{0,16},{8,24},{16,32},{24,40},{32,48},{40,56},{48,64},{56,72},{64,... | collective-permute-start | bytes 1769480 | tf_op jit(solution)/shard_map/ppermute | solution.py:284
  237.1 23.7 %collective-permute-start.4 = (f32[384,384]{1,0:T(8,128)S(1)}, f32[384,384]{1,0:T(8,128)S(1)}, u32[]{:S(2)}, u32[]{:S(2)}) collective-permute-start(f32[384,384]{1,0:T(8,128)S(1)} %get-tuple-element.28.cross_b), channel_id=1, source_target_pairs={{0,16},{8,24},{16,32},{24,40},{32,48},{40,56},{48,64},{56,72},{64,... | collective-permute-start | bytes 1769480 | tf_op jit(solution)/shard_map/ppermute | solution.py:284
  237.2 23.6 %collective-permute-start.5 = (f32[8,384]{1,0:T(8,128)S(1)}, f32[8,384]{1,0:T(8,128)S(1)}, u32[]{:S(2)}, u32[]{:S(2)}) collective-permute-start(f32[8,384]{1,0:T(8,128)S(1)} %get-tuple-element.29.vec_b), channel_id=1, source_target_pairs={{0,16},{8,24},{16,32},{24,40},{32,48},{40,56},{48,64},{56,72},{64,... | collective-permute-start | bytes 36872 | tf_op jit(solution)/shard_map/ppermute | solution.py:284
  284.7 27.8 %collective-permute-start.6 = (f32[384,384]{1,0:T(8,128)S(1)}, f32[384,384]{1,0:T(8,128)S(1)}, u32[]{:S(2)}, u32[]{:S(2)}) collective-permute-start(f32[384,384]{1,0:T(8,128)S(1)} %get-tuple-element.30.tri_b), channel_id=1, source_target_pairs={{0,32},{8,40},{16,48},{24,56},{32,64},{40,72},{48,80},{56,88},{64,... | collective-permute-start | bytes 1769480 | tf_op jit(solution)/shard_map/ppermute | solution.py:284
  287.0 25.5 %collective-permute-start.7 = (f32[384,384]{1,0:T(8,128)S(1)}, f32[384,384]{1,0:T(8,128)S(1)}, u32[]{:S(2)}, u32[]{:S(2)}) collective-permute-start(f32[384,384]{1,0:T(8,128)S(1)} %get-tuple-element.31.cross_b), channel_id=1, source_target_pairs={{0,32},{8,40},{16,48},{24,56},{32,64},{40,72},{48,80},{56,88},{64,... | collective-permute-start | bytes 1769480 | tf_op jit(solution)/shard_map/ppermute | solution.py:284
  289.1 23.4 %collective-permute-start.8 = (f32[8,384]{1,0:T(8,128)S(1)}, f32[8,384]{1,0:T(8,128)S(1)}, u32[]{:S(2)}, u32[]{:S(2)}) collective-permute-start(f32[8,384]{1,0:T(8,128)S(1)} %get-tuple-element.32.vec_b), channel_id=1, source_target_pairs={{0,32},{8,40},{16,48},{24,56},{32,64},{40,72},{48,80},{56,88},{64,... | collective-permute-start | bytes 36872 | tf_op jit(solution)/shard_map/ppermute | solution.py:284
  336.4 26.6 %collective-permute-start.9 = (f32[384,384]{1,0:T(8,128)S(1)}, f32[384,384]{1,0:T(8,128)S(1)}, u32[]{:S(2)}, u32[]{:S(2)}) collective-permute-start(f32[384,384]{1,0:T(8,128)S(1)} %get-tuple-element.33.tri_b), channel_id=1, source_target_pairs={{0,64},{8,72},{16,80},{24,88},{32,96},{40,104},{48,112},{56,120},{... | collective-permute-start | bytes 1769480 | tf_op jit(solution)/shard_map/ppermute | solution.py:284
  337.9 25.1 %collective-permute-start.10 = (f32[384,384]{1,0:T(8,128)S(1)}, f32[384,384]{1,0:T(8,128)S(1)}, u32[]{:S(2)}, u32[]{:S(2)}) collective-permute-start(f32[384,384]{1,0:T(8,128)S(1)} %get-tuple-element.34.cross_b), channel_id=1, source_target_pairs={{0,64},{8,72},{16,80},{24,88},{32,96},{40,104},{48,112},{56,120},{... | collective-permute-start | bytes 1769480 | tf_op jit(solution)/shard_map/ppermute | solution.py:284
  338.7 24.3 %collective-permute-start.11 = (f32[8,384]{1,0:T(8,128)S(1)}, f32[8,384]{1,0:T(8,128)S(1)}, u32[]{:S(2)}, u32[]{:S(2)}) collective-permute-start(f32[8,384]{1,0:T(8,128)S(1)} %get-tuple-element.35.vec_b), channel_id=1, source_target_pairs={{0,64},{8,72},{16,80},{24,88},{32,96},{40,104},{48,112},{56,120},{... | collective-permute-start | bytes 36872 | tf_op jit(solution)/shard_map/ppermute | solution.py:284
  386.9 26.0 %collective-permute-start.12 = (f32[384,384]{1,0:T(8,128)S(1)}, f32[384,384]{1,0:T(8,128)S(1)}, u32[]{:S(2)}, u32[]{:S(2)}) collective-permute-start(f32[384,384]{1,0:T(8,128)S(1)} %get-tuple-element.36.tri_b), channel_id=1, source_target_pairs={{0,128},{8,136},{16,144},{24,152},{32,160},{40,168},{48,176},{56,1... | collective-permute-start | bytes 1769480 | tf_op jit(solution)/shard_map/ppermute | solution.py:284
  387.8 25.1 %collective-permute-start.13 = (f32[384,384]{1,0:T(8,128)S(1)}, f32[384,384]{1,0:T(8,128)S(1)}, u32[]{:S(2)}, u32[]{:S(2)}) collective-permute-start(f32[384,384]{1,0:T(8,128)S(1)} %get-tuple-element.37.cross_b), channel_id=1, source_target_pairs={{0,128},{8,136},{16,144},{24,152},{32,160},{40,168},{48,176},{56,1... | collective-permute-start | bytes 1769480 | tf_op jit(solution)/shard_map/ppermute | solution.py:284
  390.4 67.7 %copy-start = (f32[3,384,384]{2,1,0:T(8,128)S(1)}, f32[3,384,384]{2,1,0:T(8,128)}, u32[]{:S(2)}) copy-start(f32[3,384,384]{2,1,0:T(8,128)} %get-tuple-element.44.ub) | copy-start | bytes 5308420
  390.4 22.4 %collective-permute-start.14 = (f32[8,384]{1,0:T(8,128)S(1)}, f32[8,384]{1,0:T(8,128)S(1)}, u32[]{:S(2)}, u32[]{:S(2)}) collective-permute-start(f32[8,384]{1,0:T(8,128)S(1)} %get-tuple-element.38.vec_b), channel_id=1, source_target_pairs={{0,128},{8,136},{16,144},{24,152},{32,160},{40,168},{48,176},{56,1... | collective-permute-start | bytes 36872 | tf_op jit(solution)/shard_map/ppermute | solution.py:284
  454.9 3.1 collective-permute-start.15
Sparse Core Ops, SparseCore 0:
  17.0 111.2 all-reduce.1
